TPU v7x, 32 devices: a whole 2x2x4 slice. The times are simulated.
32 devices in a mesh: seq: 16 (over z, x, core), head: 2 (over y).
Axes of the slice: x: 2, y: 2, z: 4, core: 2. Of those that a mesh axis runs over, the one named last changes fastest.
Arguments:
- queries: bfloat16 [16384, 2048], P(('seq', 'head')), may hold values from -6 to 6
- key_rows: bfloat16 [16384, 2048], P(('seq', 'head')), may hold values from -6 to 6
- values: bfloat16 [16384, 4096], P(('seq', 'head')), may hold values from -140 to 140
- in_gate: bfloat16 [16384, 8], P(('seq', 'head')), may hold values from -6 to 226
- forget_gate: bfloat16 [16384, 8], P(('seq', 'head')), may hold values from -0.25 to 15
- out_gate: bfloat16 [16384, 4096], P(('seq', 'head')), may hold values from -6 to 6
- norm_gain: float32 [4096], P('head'), may hold values from 0.1 to 1.9
Outputs:
- layer_out: bfloat16 [16384, 4096], P(('seq', 'head'))
All inputs are finite; a program needn't handle non-finite values.
Results may differ from a plain program's by a relative error of at most 0.0085.
Values may be sent and summed in bfloat16 or wider, within the bound.
A program may use at most 192 MiB of HBM per device.

v0:
```python
import jax
import jax.numpy as jnp
from jax import lax
from jax.sharding import PartitionSpec as P

STRETCH = 1024
far_below = -1e30
norm_eps = 1e-06


def prefix_2(part, axis, combine, identity):
    place = lax.axis_index(axis)
    gathered = jax.tree.map(lambda a: lax.all_gather(a, axis), part)
    state = jax.tree.map(lambda a, e: jnp.zeros_like(a) + jnp.asarray(e, a.dtype), part, identity)

    def one(step, state):
        return combine(
            state, jax.tree.map(lambda a: lax.dynamic_index_in_dim(a, step, 0, False), gathered)
        )

    return lax.fori_loop(0, place, one, state)


def combine(earlier, later):
    state_a, max_a, decay_a = earlier
    state_b, max_b, decay_b = later
    shifted = max_a + decay_b
    joint_max = jnp.maximum(shifted, max_b)
    state_total_sum = (
        jnp.exp(shifted - joint_max)[..., None, None] * state_a
        + jnp.exp(max_b - joint_max)[..., None, None] * state_b
    )
    return (state_total_sum, joint_max, decay_a + decay_b)


def summarize(keys_blk, values_block, in_blk, forget_blk):
    log_forget = jax.nn.log_sigmoid(forget_blk.astype(jnp.float32))
    running = jnp.cumsum(log_forget, axis=0)
    final_cum = running[-1]
    log_weight = final_cum[None, :] - running + in_blk.astype(jnp.float32)
    block_max = jnp.max(log_weight, axis=0)
    weighted_values = (
        jnp.exp(log_weight - block_max[None, :])[:, :, None] * keys_blk.astype(jnp.float32)
    ).astype(jnp.bfloat16)
    state_total_sum = jnp.einsum(
        "yij,yip->ijp", weighted_values, values_block, preferred_element_type=jnp.float32
    )
    return (running, (state_total_sum, block_max, final_cum))


def block_output(query_block, keys_blk, values_block, in_blk, running, prefix):
    prefix_state = prefix[0]
    prefix_max = prefix[1]
    scores = jnp.einsum("thk,shk->hts", query_block, keys_blk, preferred_element_type=jnp.float32)
    cum_rows = running.T
    input_rows = in_blk.astype(jnp.float32).T
    log_weight = cum_rows[:, :, None] - cum_rows[:, None, :] + input_rows[:, None, :]
    span_rows = running.shape[0]
    causal = lax.broadcasted_iota(jnp.int32, (span_rows, span_rows), 0) >= lax.broadcasted_iota(
        jnp.int32, (span_rows, span_rows), 1
    )
    log_weight = jnp.where(causal[None], log_weight, -jnp.inf)
    carried = cum_rows + prefix_max[:, None]
    row_max = jnp.maximum(carried, jnp.max(log_weight, axis=2))
    mixed_weights = (scores * jnp.exp(log_weight - row_max[:, :, None])).astype(jnp.bfloat16)
    within = jnp.einsum(
        "hts,shv->thv", mixed_weights, values_block, preferred_element_type=jnp.float32
    )
    preceding_portion = jnp.einsum(
        "ydw,dwl->ydl",
        query_block,
        prefix_state.astype(jnp.bfloat16),
        preferred_element_type=jnp.float32,
    )
    return within + jnp.exp(carried - row_max).T[:, :, None] * preceding_portion


def local(queries, key_rows, values, in_gate, forget_gate, out_gate, norm_gain):
    moved = (
        lax.all_to_all(queries, "head", split_axis=1, concat_axis=0, tiled=True),
        lax.all_to_all(key_rows, "head", split_axis=1, concat_axis=0, tiled=True),
        lax.all_to_all(values, "head", split_axis=1, concat_axis=0, tiled=True),
        lax.all_to_all(in_gate, "head", split_axis=1, concat_axis=0, tiled=True),
        lax.all_to_all(forget_gate, "head", split_axis=1, concat_axis=0, tiled=True),
        lax.all_to_all(out_gate, "head", split_axis=1, concat_axis=0, tiled=True),
    )
    gate_rows = moved[5]
    heads_here = moved[3].shape[1]
    total_rows = moved[0].shape[0]
    key_width = moved[0].shape[1] // heads_here
    value_width = moved[2].shape[1] // heads_here
    blocks = total_rows // STRETCH
    query_all = moved[0].reshape(blocks, STRETCH, heads_here, key_width)
    keys_all = moved[1].reshape(blocks, STRETCH, heads_here, key_width)
    values_all = moved[2].reshape(blocks, STRETCH, heads_here, value_width)
    input_all = moved[3].reshape(blocks, STRETCH, heads_here)
    forget_all = moved[4].reshape(blocks, STRETCH, heads_here)
    index_blk = 0
    running, summary = summarize(
        keys_all[index_blk], values_all[index_blk], input_all[index_blk], forget_all[index_blk]
    )
    running_list = [running]
    identity = (
        jnp.zeros((heads_here, key_width, value_width), jnp.float32),
        jnp.full((heads_here,), far_below, jnp.float32),
        jnp.zeros((heads_here,), jnp.float32),
    )
    prefix = prefix_2(summary, "seq", combine, identity)
    index_blk = 0
    mixed_blk = block_output(
        query_all[index_blk],
        keys_all[index_blk],
        values_all[index_blk],
        input_all[index_blk],
        running_list[index_blk],
        prefix,
    )
    mean_sq = jnp.mean(mixed_blk * mixed_blk, axis=-1, keepdims=True)
    normed = (
        mixed_blk * lax.rsqrt(mean_sq + norm_eps) * norm_gain.reshape(heads_here, value_width)
    ).astype(jnp.bfloat16)
    normed = normed.reshape(total_rows, heads_here * value_width)
    gated = (jax.nn.sigmoid(gate_rows.astype(jnp.float32)) * normed.astype(jnp.float32)).astype(
        jnp.bfloat16
    )
    return lax.all_to_all(gated, "head", split_axis=0, concat_axis=1, tiled=True)


def solution(mesh):
    placed = (
        P(("seq", "head"), None),
        P(("seq", "head"), None),
        P(("seq", "head"), None),
        P(("seq", "head"), None),
        P(("seq", "head"), None),
        P(("seq", "head"), None),
        P("head"),
    )
    return jax.shard_map(
        local, mesh=mesh, in_specs=placed, out_specs=P(("seq", "head"), None), check_vma=False
    )
```

profile of v0, /device:TPU:27, one launch (start us, length us, event | category | flops | bytes accessed | tf_op | source)
XLA Modules:
  0.0 439.4 jit_solution(12269905239405438814)
XLA Ops:
  6.5 1.3 all_to_all.86
  7.8 3.2 all-to-all-start.3
  11.1 1.3 all_to_all.88
  12.4 1.3 all-to-all-done.3
  13.7 3.2 all-to-all-start.4
  17.0 2.9 copy.53
  19.8 2.5 copy.54
  22.3 3.8 all-to-all-start.2
  26.1 4.8 %copy.100 = bf16[64,2,8,2048]{3,2,0,1:T(8,128)(2,1)} copy(bf16[64,2,8,2048]{3,2,1,0:T(8,128)(2,1)} %bitcast.114) | data formatting | bytes 8388608 | tf_op jit(solution)/shard_map/all_to_all | solution.py:82
  30.9 18.3 %all-to-all-done.2 = bf16[512,2,1024]{2,0,1:T(8,128)(2,1)S(1)} async-done(((bf16[512,2,1024]{2,0,1:T(8,128)(2,1)}), bf16[512,2,1024]{2,0,1:T(8,128)(2,1)S(1)}, u32[]{:S(2)}, u32[]{:S(2)}) %all-to-all-start.2) | async-done | bytes 2097184 | tf_op jit(solution)/shard_map/all_to_all | solution.py:81
  49.2 1.3 copy-done.1
  50.5 5.6 %all-to-all-start.5 = ((bf16[512,2,2048]{2,0,1:T(8,128)(2,1)}), bf16[512,2,2048]{2,0,1:T(8,128)(2,1)}, u32[]{:S(2)}, u32[]{:S(2)}) async-start(bf16[512,2,2048]{2,0,1:T(8,128)(2,1)} %bitcast.106), calls=%async_computation.5 | async-start | bytes 8388608 | tf_op jit(solution)/shard_map/all_to_all | solution.py:82
  56.2 1.1 reduce-window.6
  57.4 0.2 slice_reduce_fusion
  57.5 0.2 reduce-window.9
  57.8 0.2 copy.59
  58.0 0.2 copy.57
  58.3 0.2 fusion.19
  58.4 0.1 subtract_exponential_fusion.2
  58.5 3.3 squeeze_reshape.12
  61.9 2.2 multiply_convert_fusion.2
  64.1 36.8 %all-to-all-done.5 = bf16[512,2,2048]{2,0,1:T(8,128)(2,1)} async-done(((bf16[512,2,2048]{2,0,1:T(8,128)(2,1)}), bf16[512,2,2048]{2,0,1:T(8,128)(2,1)}, u32[]{:S(2)}, u32[]{:S(2)}) %all-to-all-start.5) | async-done | bytes 4194336 | tf_op jit(solution)/shard_map/all_to_all | solution.py:82
  100.9 7.8 %squeeze_reshape.13 = bf16[1024,4,512]{2,1,0:T(4,128)(2,1)} reshape(bf16[2,512,2048]{2,1,0:T(8,128)(2,1)} %bitcast.20) | data formatting | bytes 8388608 | tf_op jit(solution)/shard_map/squeeze;reshape | solution.py:113
  108.7 7.5 %copy.65 = bf16[1024,4,512]{0,2,1:T(8,128)(2,1)} copy(bf16[1024,4,512]{2,1,0:T(4,128)(2,1)} %squeeze_reshape.13) | data formatting | bytes 8388608 | tf_op jit(solution)/shard_map/squeeze;reshape | solution.py:113
  116.2 5.7 %fusion.9 = f32[4,256,512]{2,1,0:T(8,128)} fusion(bf16[1024,4,512]{0,2,1:T(8,128)(2,1)} %copy.65, bf16[1024,4,256]{2,1,0:T(4,128)(2,1)} %multiply_convert_fusion.2), kind=kOutput, calls=%fused_computation.24 | convolution fusion | flops 1073741824 | bytes 8388608 | tf_op jit(solution)/shard_map/yij,yip->ijp/dot_general | solution.py:45
  122.0 1.5 copy.101
  123.5 3.8 all-to-all-start.1
  127.4 6.6 %copy.51 = bf16[512,4096]{0,1:T(8,128)(2,1)} copy(bf16[512,4096]{1,0:T(8,128)(2,1)} %param.14) | data formatting | bytes 8388608 | tf_op args[5]
  134.0 0.6 dynamic-slice
  135.2 1.3 iota_compare_fusion
  136.6 0.2 dynamic-update-slice
  136.7 30.6 %all-reduce = f32[64]{0:T(128)S(1)} all-reduce(f32[64]{0:T(128)S(1)} %dynamic-update-slice), channel_id=2, replica_groups=mesh['seq'=16,'head'=2] {'seq'}, use_global_device_ids=true, to_apply=%add | all-reduce | flops 64 | bytes 512
  167.3 0.1 reshape.114
  167.4 0.2 copy.58
  167.6 20.2 %all-gather.2 = f32[16,1,4]{2,1,0:T(1,128)S(1)} all-gather(f32[1,1,4]{2,1,0:T(1,128)S(1)} %get-tuple-element.111), channel_id=1, replica_groups=mesh['seq'=16,'head'=2] {'seq'}, dimensions={0}, use_global_device_ids=true | all-gather | bytes 272 | tf_op jit(solution)/shard_map/all_gather | solution.py:13
  187.8 5.2 %fusion.5 = f32[4,1024]{1,0:T(4,128)S(1)} fusion(f32[4,1024]{1,0:T(4,128)S(1)} %copy.58, f32[4,1024]{1,0:T(4,128)S(1)} %bitcast.118, pred[1024,1024]{1,0:T(8,128)(4,1)} %iota_compare_fusion), kind=kLoop, calls=%fused_computation.12 | loop fusion | flops 16773120 | bytes 1097728 | tf_op jit(solution)/shard_map/reduce_max | solution.py:64
  193.0 5.8 %all-to-all-start = ((bf16[512,2,2048]{0,2,1:T(8,128)(2,1)}), bf16[512,2,2048]{0,2,1:T(8,128)(2,1)}, u32[]{:S(2)}, u32[]{:S(2)}) async-start(bf16[512,2,2048]{0,2,1:T(8,128)(2,1)} %bitcast.105), calls=%async_computation | async-start | bytes 8388608 | tf_op jit(solution)/shard_map/all_to_all | solution.py:85
  198.8 2.7 squeeze_reshape.11
  201.5 91.4 %all-gather.5.cloned.1.call-done = f32[64,256,512]{2,1,0:T(8,128)} async-done(((f32[4,256,512]{2,1,0:T(8,128)}), f32[64,256,512]{2,1,0:T(8,128)}) %all-gather.5.cloned.1.call-update) | async-done | bytes 33554448 | tf_op jit(solution)/shard_map/all_gather | solution.py:13
  292.9 0.2 broadcast_in_dim.22
  293.2 39.9 %while.14 = (s32[]{:T(128)}, f32[4,256,512]{2,1,0:T(8,128)S(1)}, f32[4]{0:T(128)S(1)}, s32[]{:T(128)}, f32[16,4]{1,0:T(8,128)S(1)}, /*index=5*/f32[16,4]{1,0:T(8...) while((s32[]{:T(128)}, f32[4,256,512]{2,1,0:T(8,128)S(1)}, f32[4]{0:T(128)S(1)}, ...), condition=%wide.region_4.5_spmd, body=%wide.region_3.4_spmd.sunk | while | flops 1572885 | bytes 6291763 | solution.py:21
  293.3 2.6 fusion.27
  296.0 2.6 fusion.27
  298.6 2.6 fusion.27
  301.3 2.6 fusion.27
  303.9 2.6 fusion.27
  306.6 2.6 fusion.27
  309.2 2.6 fusion.27
  311.9 2.6 fusion.27
  314.5 2.6 fusion.27
  317.2 2.6 fusion.27
  319.8 2.6 fusion.27
  322.5 2.6 fusion.27
  325.1 2.6 fusion.27
  327.7 2.6 fusion.27
  330.4 2.6 fusion.27
  333.2 0.1 exponential_bitcast_fusion
  333.3 14.9 %fusion.13 = f32[4,1024,512]{1,2,0:T(8,128)} fusion(bf16[1024,4,512]{0,2,1:T(8,128)(2,1)} %copy.65, f32[4,1024]{1,0:T(4,128)S(1)} %get-tuple-element.113, f32[4,1024]{1,0:T(4,128)S(1)} %copy.58, f32[4,1024]{1,0:T(4,128)S(1)} %bitcast.119, pred[1024,1024]{1,0:T(8,128)(4,1)S(1)} %copy-done.2, bf16[1024,4,256]{2,1,0:T(4,128)(2,1)} %copy-done, ...), kind=kOutput, calls=%fused_computation.27 | convolution fusion | flops 6467616768 | bytes 17874944 | tf_op jit(solution)/shard_map/hts,shv->thv/dot_general | solution.py:66
  348.2 6.2 %multiply_reduce_fusion = (f32[1024,4]{0,1:T(4,128)S(1)}, f32[1024,4,512]{0,2,1:T(8,128)S(1)}) fusion(bf16[1024,4,256]{2,1,0:T(4,128)(2,1)} %squeeze_reshape.11, f32[4,256,512]{2,1,0:T(8,128)S(1)} %get-tuple-element.65, f32[1024,4]{0,1:T(4,128)S(1)} %get-tuple-element.112, f32[4,1024,512]{1,2,0:T(8,128)} %fusion.13), kind=kOutput, calls=%fused_computation.18 | convolution fusion | flops 1082650624 | bytes 21004288 | tf_op jit(solution)/shard_map/ydw,dwl->ydl/dot_general | solution.py:69
  354.4 4.0 fusion.8
  358.4 11.8 %reshape.113 = f32[2,512,2048]{1,0,2:T(2,128)} reshape(f32[1024,4,512]{0,2,1:T(8,128)} %fusion.8) | data formatting | bytes 16777216 | tf_op jit(solution)/shard_map/convert_element_type | solution.py:123
  370.2 6.7 %fusion.7 = bf16[2,512,2048]{1,2,0:T(8,128)(2,1)S(1)} fusion(f32[2,512,2048]{1,0,2:T(2,128)} %reshape.113, bf16[512,2,2048]{0,2,1:T(8,128)(2,1)} %all-to-all-done), kind=kLoop, calls=%fused_computation.16 | loop fusion | flops 12582912 | bytes 16777216 | tf_op jit(solution)/shard_map/convert_element_type | solution.py:123
  376.8 49.4 %all_to_all.103 = bf16[2,512,2048]{1,2,0:T(8,128)(2,1)} all-to-all(bf16[2,512,2048]{1,2,0:T(8,128)(2,1)S(1)} %fusion.7), channel_id=1, replica_groups=mesh['seq'=16,'head'=2] {'head'}, dimensions={0} | all-to-all | bytes 8388608 | tf_op jit(solution)/shard_map/all_to_all | solution.py:126
  426.2 6.3 %copy.69 = bf16[512,4096]{1,0:T(8,128)(2,1)} copy(bf16[512,4096]{0,1:T(8,128)(2,1)} %bitcast.107) | data formatting | bytes 8388608 | tf_op jit(solution)/shard_map/all_to_all | solution.py:126
  (57 shorter events, 0.8 us)
Async XLA Ops:
  7.8 5.9 %all-to-all-start.3 = ((bf16[512,2,4]{0,2,1:T(4,128)(2,1)}), bf16[512,2,4]{0,2,1:T(4,128)(2,1)S(1)}, u32[]{:S(2)}, u32[]{:S(2)}) async-start(bf16[512,2,4]{0,2,1:T(4,128)(2,1)} %all_to_all.86), calls=%async_computation.3 | async-start | bytes 16384 | tf_op jit(solution)/shard_map/all_to_all | solution.py:84
  13.7 8.6 %all-to-all-start.4 = ((bf16[512,2,4]{0,2,1:T(4,128)(2,1)}), bf16[512,2,4]{0,2,1:T(4,128)(2,1)S(1)}, u32[]{:S(2)}, u32[]{:S(2)}) async-start(bf16[512,2,4]{0,2,1:T(4,128)(2,1)} %all_to_all.88), calls=%async_computation.4 | async-start | bytes 16384 | tf_op jit(solution)/shard_map/all_to_all | solution.py:83
  22.3 26.9 %all-to-all-start.2 = ((bf16[512,2,1024]{2,0,1:T(8,128)(2,1)}), bf16[512,2,1024]{2,0,1:T(8,128)(2,1)S(1)}, u32[]{:S(2)}, u32[]{:S(2)}) async-start(bf16[512,2,1024]{2,0,1:T(8,128)(2,1)} %copy.54), calls=%async_computation.2 | async-start | bytes 4194304 | tf_op jit(solution)/shard_map/all_to_all | solution.py:81
  49.2 1.3 copy-start.1
  50.5 50.4 %all-to-all-start.5 = ((bf16[512,2,2048]{2,0,1:T(8,128)(2,1)}), bf16[512,2,2048]{2,0,1:T(8,128)(2,1)}, u32[]{:S(2)}, u32[]{:S(2)}) async-start(bf16[512,2,2048]{2,0,1:T(8,128)(2,1)} %bitcast.106), calls=%async_computation.5 | async-start | bytes 8388608 | tf_op jit(solution)/shard_map/all_to_all | solution.py:82
  56.1 236.8 %all-gather.5.cloned.1.call-start = ((), (), s32[]{:S(2)}) async-start(), calls=%async_computation.7 | async-start | bytes 35651584 | tf_op jit(solution)/shard_map/all_gather | solution.py:13
  61.9 46.9 %copy-start = (bf16[1024,4,256]{2,1,0:T(4,128)(2,1)}, bf16[1024,4,256]{2,1,0:T(4,128)(2,1)S(1)}, u32[]{:S(2)}) copy-start(bf16[1024,4,256]{2,1,0:T(4,128)(2,1)S(1)} %squeeze_reshape.12) | copy-start | bytes 6291460
  116.2 5.8 %copy-start.3 = (bf16[512,2048]{1,0:T(8,128)(2,1)S(1)}, bf16[512,2048]{1,0:T(8,128)(2,1)}, u32[]{:S(2)}) copy-start(bf16[512,2048]{1,0:T(8,128)(2,1)} %param.9) | copy-start | bytes 6291460
  122.0 5.3 %copy-start.4 = (f32[2048]{0:T(1024)S(1)}, f32[2048]{0:T(1024)}, u32[]{:S(2)}) copy-start(f32[2048]{0:T(1024)} %param.15) | copy-start | bytes 24580
  123.5 69.4 %all-to-all-start.1 = ((bf16[512,2,1024]{2,0,1:T(8,128)(2,1)}), bf16[512,2,1024]{2,0,1:T(8,128)(2,1)S(1)}, u32[]{:S(2)}, u32[]{:S(2)}) async-start(bf16[512,2,1024]{2,0,1:T(8,128)(2,1)} %bitcast.110), calls=%async_computation.1 | async-start | bytes 4194304 | tf_op jit(solution)/shard_map/all_to_all | solution.py:80
  127.3 6.6 %copy-start.5 = (u32[32]{0:T(128)S(1)}, u32[32]{0:T(128)}, u32[]{:S(2)}) copy-start(u32[32]{0:T(128)} %constant.48) | copy-start | bytes 388
  193.0 177.2 %all-to-all-start = ((bf16[512,2,2048]{0,2,1:T(8,128)(2,1)}), bf16[512,2,2048]{0,2,1:T(8,128)(2,1)}, u32[]{:S(2)}, u32[]{:S(2)}) async-start(bf16[512,2,2048]{0,2,1:T(8,128)(2,1)} %bitcast.105), calls=%async_computation | async-start | bytes 8388608 | tf_op jit(solution)/shard_map/all_to_all | solution.py:85
  293.2 40.1 %copy-start.2 = (pred[1024,1024]{1,0:T(8,128)(4,1)S(1)}, pred[1024,1024]{1,0:T(8,128)(4,1)}, u32[]{:S(2)}) copy-start(pred[1024,1024]{1,0:T(8,128)(4,1)} %iota_compare_fusion) | copy-start | bytes 3145732
Sparse Core Ops, SparseCore 0:
  122.1 170.7 all-gather.4
where the time goes:
time: 441 us; the launch traced here: 439 us
  waiting for transfers between devices  148 us (34%)
  blocking collectives  100 us (23%)
  local copies, waits for them, and re-layouts  63.7 us (14%)
  other arithmetic  60.4 us (14%)
  matrix products  26.8 us (6%)
  starting transfers between devices  25.4 us (6%)
  between operations  14.3 us (3%)
    all_gather x1, waiting for transfers between devices, prefix_2(): gathered = jax.tree.map(lambda a: lax.all_gather(a, axis), part)  91.4 us
    all_to_all x1, blocking collectives, local(): lax.all_to_all(gated, 'head', split_axis=0, concat_axis=1, tiled=True)  49.4 us
    add x15, other arithmetic, combine(): jnp.exp(shifted - joint_max)[..., None, None] * state_a  38.7 us
    all_to_all x1, waiting for transfers between devices, local(): lax.all_to_all(values, 'head', split_axis=1, concat_axis=0, tiled=True)  36.8 us
    unnamed x1, blocking collectives  30.6 us
    all_gather x1, blocking collectives, prefix_2(): gathered = jax.tree.map(lambda a: lax.all_gather(a, axis), part)  20.2 us
    all_to_all x1, waiting for transfers between devices, local(): lax.all_to_all(key_rows, 'head', split_axis=1, concat_axis=0, tiled=True)  18.3 us
    another operation x2, local copies, waits for them, and re-layouts, local(): values_all[index_blk]  15.3 us
  transfers between devices with their start and end apart: 7, of which 4 were waited for; matrix products, arithmetic and copies ran while one was open for 26% of the time, Pallas kernels for 0%

commit v1 on v0

--- a/solution.py
+++ b/solution.py
@@ -6,6 +6,13 @@
 STRETCH = 1024
 far_below = -1e30
 norm_eps = 1e-06
+
+
+def exchange_blocks(x, axis, split, join):
+    size = lax.axis_size(axis)
+    blocks = jnp.stack(jnp.split(x, size, axis=split), axis=0)
+    blocks = lax.all_to_all(blocks, axis, split_axis=0, concat_axis=0)
+    return jnp.concatenate(blocks, axis=join)
 
 
 def prefix_2(part, axis, combine, identity):
@@ -123,7 +130,7 @@
     gated = (jax.nn.sigmoid(gate_rows.astype(jnp.float32)) * normed.astype(jnp.float32)).astype(
         jnp.bfloat16
     )
-    return lax.all_to_all(gated, "head", split_axis=0, concat_axis=1, tiled=True)
+    return exchange_blocks(gated, "head", 0, 1)
 
 
 def solution(mesh):

time: 441 us -> 426 us (0.966)
  waiting for transfers between devices: 148 us -> 125 us
    all_gather x1, waiting for transfers between devices: 91.4 us -> 59.6 us  [prefix_2(): gathered = jax.tree.map(lambda a: lax.all_gather(a, axis), part)]
    convert_element_type x1 -> x0, local copies, waits for them, and re-layouts: 11.8 us -> none  [local(): normed.astype(jnp.float32)]
    div x0 -> x1, local copies, waits for them, and re-layouts: none -> 9.32 us  [local(): jax.nn.sigmoid(gate_rows.astype(jnp.float32)) * normed.astype(jnp.float32)]
    all_to_all x1, waiting for transfers between devices: 0.01 us -> 8.56 us  [local(): lax.all_to_all(queries, 'head', split_axis=1, concat_axis=0, tiled=True)]
    div x0 -> x1, other arithmetic: none -> 7.63 us  [local(): jax.nn.sigmoid(gate_rows.astype(jnp.float32)) * normed.astype(jnp.float32)]
    reshape x0 -> x1, local copies, waits for them, and re-layouts: none -> 6.32 us  [exchange_blocks(): return jnp.concatenate(blocks, axis=join)]
  transfers between devices with their start and end apart: 7 -> 7, of which waited for: 4 -> 5; matrix products, arithmetic and copies ran while one was open for 26% -> 14% of each run, Pallas kernels for 0% -> 0%
where the time goes in v1:
time: 426 us; the launch traced here: 424 us
  waiting for transfers between devices  125 us (29%)
  blocking collectives  100 us (23%)
  local copies, waits for them, and re-layouts  67.9 us (16%)
  other arithmetic  63.5 us (15%)
  matrix products  26.8 us (6%)
  starting transfers between devices  25.3 us (6%)
  between operations  14.3 us (3%)
    all_gather x1, waiting for transfers between devices, prefix_2(): gathered = jax.tree.map(lambda a: lax.all_gather(a, axis), part)  59.6 us
    all_to_all x1, blocking collectives, exchange_blocks(): blocks = lax.all_to_all(blocks, axis, split_axis=0, concat_axis=0)  49.4 us
    add x15, other arithmetic, combine(): jnp.exp(shifted - joint_max)[..., None, None] * state_a  38.7 us
    all_to_all x1, waiting for transfers between devices, local(): lax.all_to_all(values, 'head', split_axis=1, concat_axis=0, tiled=True)  36.8 us
    unnamed x1, blocking collectives  30.6 us
    all_gather x1, blocking collectives, prefix_2(): gathered = jax.tree.map(lambda a: lax.all_gather(a, axis), part)  20.4 us
    all_to_all x1, waiting for transfers between devices, local(): lax.all_to_all(key_rows, 'head', split_axis=1, concat_axis=0, tiled=True)  18.3 us
    another operation x2, local copies, waits for them, and re-layouts, local(): values_all[index_blk]  15.3 us
  transfers between devices with their start and end apart: 7, of which 5 were waited for; matrix products, arithmetic and copies ran while one was open for 14% of the time, Pallas kernels for 0%

profile of v1, /device:TPU:27, one launch (start us, length us, event | category | flops | bytes accessed | tf_op | source)
XLA Modules:
  0.0 423.5 jit_solution(12279987506252182197)
XLA Ops:
  6.5 1.3 all_to_all.77
  7.8 3.2 all-to-all-start.3
  11.1 1.3 all_to_all.79
  12.4 1.4 all-to-all-done.3
  13.7 3.2 all-to-all-start.4
  16.9 2.9 copy.53
  19.8 2.5 copy.54
  22.3 3.8 all-to-all-start.2
  26.1 4.8 %copy.100 = bf16[64,2,8,2048]{3,2,0,1:T(8,128)(2,1)} copy(bf16[64,2,8,2048]{3,2,1,0:T(8,128)(2,1)} %bitcast.119) | data formatting | bytes 8388608 | tf_op jit(solution)/shard_map/all_to_all | solution.py:89
  30.9 18.3 %all-to-all-done.2 = bf16[512,2,1024]{2,0,1:T(8,128)(2,1)S(1)} async-done(((bf16[512,2,1024]{2,0,1:T(8,128)(2,1)}), bf16[512,2,1024]{2,0,1:T(8,128)(2,1)S(1)}, u32[]{:S(2)}, u32[]{:S(2)}) %all-to-all-start.2) | async-done | bytes 2097184 | tf_op jit(solution)/shard_map/all_to_all | solution.py:88
  49.2 1.3 copy-done.1
  50.5 5.6 %all-to-all-start.5 = ((bf16[512,2,2048]{2,0,1:T(8,128)(2,1)}), bf16[512,2,2048]{2,0,1:T(8,128)(2,1)}, u32[]{:S(2)}, u32[]{:S(2)}) async-start(bf16[512,2,2048]{2,0,1:T(8,128)(2,1)} %bitcast.110), calls=%async_computation.5 | async-start | bytes 8388608 | tf_op jit(solution)/shard_map/all_to_all | solution.py:89
  56.2 1.1 reduce-window.6
  57.5 0.2 reduce-window.9
  57.8 0.2 copy.59
  58.1 0.2 copy.57
  58.6 3.3 squeeze_reshape.12
  61.9 2.2 multiply_convert_fusion.2
  64.1 36.8 %all-to-all-done.5 = bf16[512,2,2048]{2,0,1:T(8,128)(2,1)} async-done(((bf16[512,2,2048]{2,0,1:T(8,128)(2,1)}), bf16[512,2,2048]{2,0,1:T(8,128)(2,1)}, u32[]{:S(2)}, u32[]{:S(2)}) %all-to-all-start.5) | async-done | bytes 4194336 | tf_op jit(solution)/shard_map/all_to_all | solution.py:89
  100.9 7.8 %squeeze_reshape.13 = bf16[1024,4,512]{2,1,0:T(4,128)(2,1)} reshape(bf16[2,512,2048]{2,1,0:T(8,128)(2,1)} %bitcast.21) | data formatting | bytes 8388608 | tf_op jit(solution)/shard_map/squeeze;reshape | solution.py:120
  108.7 7.5 %copy.65 = bf16[1024,4,512]{0,2,1:T(8,128)(2,1)} copy(bf16[1024,4,512]{2,1,0:T(4,128)(2,1)} %squeeze_reshape.13) | data formatting | bytes 8388608 | tf_op jit(solution)/shard_map/squeeze;reshape | solution.py:120
  116.3 5.7 %fusion.8 = f32[4,256,512]{2,1,0:T(8,128)} fusion(bf16[1024,4,512]{0,2,1:T(8,128)(2,1)} %copy.65, bf16[1024,4,256]{2,1,0:T(4,128)(2,1)} %multiply_convert_fusion.2), kind=kOutput, calls=%fused_computation.27 | convolution fusion | flops 1073741824 | bytes 8388608 | tf_op jit(solution)/shard_map/yij,yip->ijp/dot_general | solution.py:52
  122.0 1.5 copy.101
  123.6 3.8 all-to-all-start.1
  127.3 6.6 %copy.50 = bf16[512,4096]{0,1:T(8,128)(2,1)} copy(bf16[512,4096]{1,0:T(8,128)(2,1)} %param.14) | data formatting | bytes 8388608 | tf_op args[5]
  133.9 6.3 %copy.51 = bf16[512,2,2048]{2,0,1:T(8,128)(2,1)} copy(bf16[512,2,2048]{0,2,1:T(8,128)(2,1)} %bitcast.112) | data formatting | bytes 8388608 | tf_op jit(solution)/shard_map/all_to_all | solution.py:92
  140.3 8.6 %all-to-all-done.1 = bf16[512,2,1024]{2,0,1:T(8,128)(2,1)S(1)} async-done(((bf16[512,2,1024]{2,0,1:T(8,128)(2,1)}), bf16[512,2,1024]{2,0,1:T(8,128)(2,1)S(1)}, u32[]{:S(2)}, u32[]{:S(2)}) %all-to-all-start.1) | async-done | bytes 2097184 | tf_op jit(solution)/shard_map/all_to_all | solution.py:87
  148.8 5.6 %all-to-all-start = ((bf16[512,2,2048]{2,0,1:T(8,128)(2,1)}), bf16[512,2,2048]{2,0,1:T(8,128)(2,1)}, u32[]{:S(2)}, u32[]{:S(2)}) async-start(bf16[512,2,2048]{2,0,1:T(8,128)(2,1)} %copy.51), calls=%async_computation | async-start | bytes 8388608 | tf_op jit(solution)/shard_map/all_to_all | solution.py:92
  154.5 0.6 dynamic-slice
  155.7 1.3 iota_compare_fusion
  157.0 0.2 dynamic-update-slice
  157.2 30.6 %all-reduce = f32[64]{0:T(128)S(1)} all-reduce(f32[64]{0:T(128)S(1)} %dynamic-update-slice), channel_id=2, replica_groups=mesh['seq'=16,'head'=2] {'seq'}, use_global_device_ids=true, to_apply=%add | all-reduce | flops 64 | bytes 512
  187.9 0.2 copy.58
  188.0 20.4 %all-gather.2 = f32[16,1,4]{2,1,0:T(1,128)S(1)} all-gather(f32[1,1,4]{2,1,0:T(1,128)S(1)} %get-tuple-element.113), channel_id=1, replica_groups=mesh['seq'=16,'head'=2] {'seq'}, dimensions={0}, use_global_device_ids=true | all-gather | bytes 272 | tf_op jit(solution)/shard_map/all_gather | solution.py:20
  208.5 5.2 %fusion.5 = f32[4,1024]{1,0:T(4,128)S(1)} fusion(f32[4,1024]{1,0:T(4,128)S(1)} %copy.58, f32[4,1024]{1,0:T(4,128)S(1)} %bitcast.123, pred[1024,1024]{1,0:T(8,128)(4,1)} %iota_compare_fusion), kind=kLoop, calls=%fused_computation.12 | loop fusion | flops 16773120 | bytes 1097728 | tf_op jit(solution)/shard_map/reduce_max | solution.py:71
  213.7 2.8 squeeze_reshape.11
  216.4 7.6 %add_divide_fusion = f32[512,2,2048]{2,0,1:T(8,128)} fusion(bf16[512,2,2048]{2,0,1:T(8,128)(2,1)} %all-to-all-done), kind=kLoop, calls=%fused_computation.17 | loop fusion | flops 8388608 | bytes 12582912 | tf_op jit(solution)/shard_map/div | solution.py:130
  224.0 9.3 %copy.68 = f32[1024,2048]{0,1:T(8,128)} copy(f32[1024,2048]{1,0:T(8,128)} %bitcast.109) | data formatting | bytes 16777216 | tf_op jit(solution)/shard_map/div | solution.py:130
  233.4 59.6 %all-gather.5.cloned.1.call-done = f32[64,256,512]{2,1,0:T(8,128)} async-done(((f32[4,256,512]{2,1,0:T(8,128)}), f32[64,256,512]{2,1,0:T(8,128)}) %all-gather.5.cloned.1.call-update) | async-done | bytes 33554448 | tf_op jit(solution)/shard_map/all_gather | solution.py:20
  292.9 0.2 broadcast_in_dim.22
  293.2 40.0 %while.14 = (s32[]{:T(128)}, f32[4,256,512]{2,1,0:T(8,128)S(1)}, f32[4]{0:T(128)S(1)}, s32[]{:T(128)}, f32[16,4]{1,0:T(8,128)S(1)}, /*index=5*/f32[16,4]{1,0:T(8...) while((s32[]{:T(128)}, f32[4,256,512]{2,1,0:T(8,128)S(1)}, f32[4]{0:T(128)S(1)}, ...), condition=%wide.region_4.5_spmd, body=%wide.region_3.4_spmd.sunk | while | flops 1572885 | bytes 6291763 | solution.py:28
  293.3 2.6 fusion.26
  296.0 2.6 fusion.26
  298.6 2.6 fusion.26
  301.3 2.6 fusion.26
  303.9 2.6 fusion.26
  306.6 2.6 fusion.26
  309.2 2.6 fusion.26
  311.8 2.6 fusion.26
  314.5 2.6 fusion.26
  317.1 2.6 fusion.26
  319.8 2.6 fusion.26
  322.4 2.6 fusion.26
  325.1 2.6 fusion.26
  327.7 2.6 fusion.26
  330.3 2.6 fusion.26
  333.3 14.9 %fusion.12 = f32[4,1024,512]{1,2,0:T(8,128)} fusion(bf16[1024,4,512]{0,2,1:T(8,128)(2,1)} %copy.65, f32[4,1024]{1,0:T(4,128)S(1)} %get-tuple-element.115, f32[4,1024]{1,0:T(4,128)S(1)} %copy.58, f32[4,1024]{1,0:T(4,128)S(1)} %bitcast.124, pred[1024,1024]{1,0:T(8,128)(4,1)S(1)} %copy-done.2, bf16[1024,4,256]{2,1,0:T(4,128)(2,1)} %copy-done, ...), kind=kOutput, calls=%fused_computation.30 | convolution fusion | flops 6467616768 | bytes 17874944 | tf_op jit(solution)/shard_map/hts,shv->thv/dot_general | solution.py:73
  348.2 6.2 %multiply_reduce_fusion = (f32[1024,4]{0,1:T(4,128)S(1)}, f32[1024,4,512]{0,2,1:T(8,128)S(1)}) fusion(bf16[1024,4,256]{2,1,0:T(4,128)(2,1)} %squeeze_reshape.11, f32[4,256,512]{2,1,0:T(8,128)S(1)} %get-tuple-element.65, f32[1024,4]{0,1:T(4,128)S(1)} %get-tuple-element.114, f32[4,1024,512]{1,2,0:T(8,128)} %fusion.12), kind=kOutput, calls=%fused_computation.19 | convolution fusion | flops 1082650624 | bytes 21004288 | tf_op jit(solution)/shard_map/ydw,dwl->ydl/dot_general | solution.py:76
  354.4 0.8 multiply_convert_fusion.1
  355.2 5.0 %fusion.6 = bf16[1024,2048]{0,1:T(8,128)(2,1)S(1)} fusion(f32[1024,2048]{0,1:T(8,128)} %copy.68, bf16[1024,4,512]{0,2,1:T(8,128)(2,1)S(1)} %multiply_convert_fusion.1), kind=kLoop, calls=%fused_computation.14 | loop fusion | flops 6291456 | bytes 16777216 | tf_op jit(solution)/shard_map/convert_element_type | solution.py:130
  360.2 0.3 slice_bitcast_fusion.1
  360.6 0.4 pad_maximum_fusion
  361.0 49.4 %all_to_all.92 = bf16[2,512,2048]{1,2,0:T(8,128)(2,1)} all-to-all(bf16[2,512,2048]{1,2,0:T(8,128)(2,1)S(1)} %pad_maximum_fusion), channel_id=1, replica_groups=mesh['seq'=16,'head'=2] {'head'}, dimensions={0} | all-to-all | bytes 8388608 | tf_op jit(solution)/shard_map/all_to_all | solution.py:14
  410.4 6.3 %copy.72 = bf16[512,4096]{1,0:T(8,128)(2,1)} copy(bf16[512,4096]{0,1:T(8,128)(2,1)} %bitcast.111) | data formatting | bytes 8388608 | tf_op jit(solution)/shard_map/reshape | solution.py:15
  (61 shorter events, 1.3 us)
Async XLA Ops:
  7.8 5.9 %all-to-all-start.3 = ((bf16[512,2,4]{0,2,1:T(4,128)(2,1)}), bf16[512,2,4]{0,2,1:T(4,128)(2,1)S(1)}, u32[]{:S(2)}, u32[]{:S(2)}) async-start(bf16[512,2,4]{0,2,1:T(4,128)(2,1)} %all_to_all.77), calls=%async_computation.3 | async-start | bytes 16384 | tf_op jit(solution)/shard_map/all_to_all | solution.py:91
  13.7 8.6 %all-to-all-start.4 = ((bf16[512,2,4]{0,2,1:T(4,128)(2,1)}), bf16[512,2,4]{0,2,1:T(4,128)(2,1)S(1)}, u32[]{:S(2)}, u32[]{:S(2)}) async-start(bf16[512,2,4]{0,2,1:T(4,128)(2,1)} %all_to_all.79), calls=%async_computation.4 | async-start | bytes 16384 | tf_op jit(solution)/shard_map/all_to_all | solution.py:90
  22.3 26.9 %all-to-all-start.2 = ((bf16[512,2,1024]{2,0,1:T(8,128)(2,1)}), bf16[512,2,1024]{2,0,1:T(8,128)(2,1)S(1)}, u32[]{:S(2)}, u32[]{:S(2)}) async-start(bf16[512,2,1024]{2,0,1:T(8,128)(2,1)} %copy.54), calls=%async_computation.2 | async-start | bytes 4194304 | tf_op jit(solution)/shard_map/all_to_all | solution.py:88
  49.2 1.3 copy-start.1
  50.5 50.4 %all-to-all-start.5 = ((bf16[512,2,2048]{2,0,1:T(8,128)(2,1)}), bf16[512,2,2048]{2,0,1:T(8,128)(2,1)}, u32[]{:S(2)}, u32[]{:S(2)}) async-start(bf16[512,2,2048]{2,0,1:T(8,128)(2,1)} %bitcast.110), calls=%async_computation.5 | async-start | bytes 8388608 | tf_op jit(solution)/shard_map/all_to_all | solution.py:89
  56.1 236.8 %all-gather.5.cloned.1.call-start = ((), (), s32[]{:S(2)}) async-start(), calls=%async_computation.7 | async-start | bytes 35651584 | tf_op jit(solution)/shard_map/all_gather | solution.py:20
  61.9 46.9 %copy-start = (bf16[1024,4,256]{2,1,0:T(4,128)(2,1)}, bf16[1024,4,256]{2,1,0:T(4,128)(2,1)S(1)}, u32[]{:S(2)}) copy-start(bf16[1024,4,256]{2,1,0:T(4,128)(2,1)S(1)} %squeeze_reshape.12) | copy-start | bytes 6291460
  116.3 5.8 %copy-start.3 = (bf16[512,2048]{1,0:T(8,128)(2,1)S(1)}, bf16[512,2048]{1,0:T(8,128)(2,1)}, u32[]{:S(2)}) copy-start(bf16[512,2048]{1,0:T(8,128)(2,1)} %param.9) | copy-start | bytes 6291460
  123.6 25.2 %all-to-all-start.1 = ((bf16[512,2,1024]{2,0,1:T(8,128)(2,1)}), bf16[512,2,1024]{2,0,1:T(8,128)(2,1)S(1)}, u32[]{:S(2)}, u32[]{:S(2)}) async-start(bf16[512,2,1024]{2,0,1:T(8,128)(2,1)} %bitcast.115), calls=%async_computation.1 | async-start | bytes 4194304 | tf_op jit(solution)/shard_map/all_to_all | solution.py:87
  140.2 14.2 %copy-start.4 = (f32[2048]{0:T(1024)S(1)}, f32[2048]{0:T(1024)}, u32[]{:S(2)}) copy-start(f32[2048]{0:T(1024)} %param.15) | copy-start | bytes 24580
  140.2 14.2 %copy-start.5 = (u32[32]{0:T(128)S(1)}, u32[32]{0:T(128)}, u32[]{:S(2)}) copy-start(u32[32]{0:T(128)} %constant.48) | copy-start | bytes 388
  148.8 67.6 %all-to-all-start = ((bf16[512,2,2048]{2,0,1:T(8,128)(2,1)}), bf16[512,2,2048]{2,0,1:T(8,128)(2,1)}, u32[]{:S(2)}, u32[]{:S(2)}) async-start(bf16[512,2,2048]{2,0,1:T(8,128)(2,1)} %copy.51), calls=%async_computation | async-start | bytes 8388608 | tf_op jit(solution)/shard_map/all_to_all | solution.py:92
  293.2 40.1 %copy-start.2 = (pred[1024,1024]{1,0:T(8,128)(4,1)S(1)}, pred[1024,1024]{1,0:T(8,128)(4,1)}, u32[]{:S(2)}) copy-start(pred[1024,1024]{1,0:T(8,128)(4,1)} %iota_compare_fusion) | copy-start | bytes 3145732
Sparse Core Ops, SparseCore 0:
  122.1 170.7 all-gather.4
